TPU v7x, 256 devices: a whole 4x4x8 slice. The times are simulated.
256 devices in a mesh: wa: 16 (over y_hi, z), dev: 16 (over y_lo, x, core).
Axes of the slice: x: 4, y: 4 (y_hi: 2, y_lo: 2; y = y_hi * 2 + y_lo), z: 8, core: 2. Of those that a mesh axis runs over, the one named last changes fastest.
Arguments:
- output_gradient: bfloat16 [2048, 8192], P('wa'), may hold values from -6 to 6
- down_weight: bfloat16 [28672, 8192], P('dev', 'wa'), may hold values from -0.03125 to 0.03125
- gate_preactivation: bfloat16 [2048, 28672], P('wa', 'dev'), may hold values from -6 to 6
- up_preactivation: bfloat16 [2048, 28672], P('wa', 'dev'), may hold values from -6 to 6
- adapter_down_factor: bfloat16 [16, 16, 28672], P(None, None, 'dev'), may hold values from -0.0625 to 0.0625
- adapter_up_factor: bfloat16 [16, 16, 8192], P(None, None, 'dev'), may hold values from -0.0625 to 0.0625
- tile_owner_adapter: int32 [128, 1], replicated, may hold values from 0 to 15
- tile_live_count: int32 [128], replicated, may hold values from 1 to 16
Outputs:
- grad_gate: bfloat16 [2048, 28672], P('wa', 'dev')
- grad_up: bfloat16 [2048, 28672], P('wa', 'dev')
- grad_a: float32 [16, 16, 28672], P('wa', None, 'dev')
- grad_b: float32 [16, 16, 8192], P('wa', None, 'dev')
Inputs may be any that keep to these rules, and one draw needn't show every extreme that they name: `tile_owner_adapter`: every one of the 16 adapters owns at least one tile.
All inputs are finite; a program needn't handle non-finite values.
Results may differ from a plain program's by a relative error of at most 0.013.
Values may be sent and summed in bfloat16 or wider, within the bound.
A program may use at most 128 MiB of HBM per device.

v0:
```python
import jax
import jax.numpy as jnp
from jax import lax
from jax.sharding import PartitionSpec as P

TILE = 16


def on_device(
    output_gradient,
    down_weight,
    gate_preactivation,
    up_preactivation,
    adapter_down_factor,
    adapter_up_factor,
    tile_owner_adapter,
    tile_live_count,
):
    wa_index = lax.axis_index("wa")
    dev_index = lax.axis_index("dev")
    token_rows = output_gradient.shape[0]
    hidden_local = down_weight.shape[0]
    wa_cols = down_weight.shape[1]
    shard_columns = adapter_up_factor.shape[2]
    adapter_list = adapter_down_factor.shape[0]
    adapter_rank_rows = adapter_down_factor.shape[1]
    tiles_local = token_rows // TILE
    own_adapter = lax.dynamic_slice_in_dim(
        tile_owner_adapter[:, 0], wa_index * tiles_local, tiles_local
    )
    own_live = lax.dynamic_slice_in_dim(tile_live_count, wa_index * tiles_local, tiles_local)
    row_adapter = jnp.repeat(own_adapter, TILE)
    position = jnp.arange(token_rows) % TILE
    live_rows = position < jnp.repeat(own_live, TILE)
    masked_rows = jnp.where(
        live_rows[:, None], output_gradient, jnp.zeros((), output_gradient.dtype)
    )
    gate_wide = gate_preactivation.astype(jnp.float32)
    up_wide = up_preactivation.astype(jnp.float32)
    hidden_state = (jax.nn.silu(gate_wide) * up_wide).astype(jnp.bfloat16)
    shard_piece = lax.all_gather(down_weight, "wa", axis=1, tiled=True)
    groups = shard_piece.shape[1] // wa_cols
    left = masked_rows.reshape(token_rows, groups, wa_cols)
    right = shard_piece.reshape(hidden_local, groups, wa_cols)
    partial_value = jnp.einsum("tkc,fkc->ktf", left, right, preferred_element_type=jnp.float32)
    rounded = lax.optimization_barrier(partial_value.astype(jnp.bfloat16))
    base_grad = jnp.sum(rounded.astype(jnp.float32), axis=0)
    selector = row_adapter[:, None] == jnp.arange(adapter_list, dtype=jnp.int32)[None, :]
    flattened_down = adapter_down_factor.reshape(adapter_list * adapter_rank_rows, hidden_local)
    flattened_up = adapter_up_factor.reshape(adapter_list * adapter_rank_rows, shard_columns)

    def choose_rows(complete_value):
        reshaped_value = complete_value.reshape(token_rows, adapter_list, adapter_rank_rows)
        return jnp.sum(
            jnp.where(selector[:, :, None], reshaped_value, jnp.zeros((), complete_value.dtype)),
            axis=1,
        )

    def spread_value(values):
        wide_value = jnp.where(
            selector[:, :, None], values[:, None, :], jnp.zeros((), values.dtype)
        )
        return wide_value.reshape(token_rows, adapter_list * adapter_rank_rows)

    grad_slice = lax.dynamic_slice_in_dim(masked_rows, dev_index * shard_columns, shard_columns, 1)
    in_partial = choose_rows(
        lax.dot_general(
            hidden_state,
            flattened_down,
            (((1,), (1,)), ((), ())),
            preferred_element_type=jnp.float32,
        )
    )
    out_partial = choose_rows(
        lax.dot_general(
            grad_slice, flattened_up, (((1,), (1,)), ((), ())), preferred_element_type=jnp.float32
        )
    )
    in_summed, out_summed = lax.psum((in_partial, out_partial), "dev")
    spread_input = spread_value(in_summed.astype(jnp.bfloat16))
    spread_output = spread_value(out_summed.astype(jnp.bfloat16))
    hidden_grad = base_grad + 2.0 * jnp.dot(
        spread_output, flattened_down, preferred_element_type=jnp.float32
    )
    sigmoid_gate = jax.nn.sigmoid(gate_wide)
    grad_up = (hidden_grad * gate_wide * sigmoid_gate).astype(jnp.bfloat16)
    grad_gate = (
        hidden_grad * up_wide * sigmoid_gate * (1.0 + gate_wide * (1.0 - sigmoid_gate))
    ).astype(jnp.bfloat16)
    down_factor_partial = 2.0 * lax.dot_general(
        spread_output, hidden_state, (((0,), (0,)), ((), ())), preferred_element_type=jnp.float32
    )
    up_factor_partial = 2.0 * lax.dot_general(
        spread_input, grad_slice, (((0,), (0,)), ((), ())), preferred_element_type=jnp.float32
    )
    down_factor_partial = down_factor_partial.reshape(adapter_list, adapter_rank_rows, hidden_local)
    up_factor_partial = up_factor_partial.reshape(adapter_list, adapter_rank_rows, shard_columns)
    grad_a, grad_b = (
        lax.psum_scatter(down_factor_partial, "wa", scatter_dimension=0, tiled=True),
        lax.psum_scatter(up_factor_partial, "wa", scatter_dimension=0, tiled=True),
    )
    return (grad_gate, grad_up, grad_a, grad_b)


def solution(mesh):
    placed = (
        P("wa", None),
        P("dev", "wa"),
        P("wa", "dev"),
        P("wa", "dev"),
        P(None, None, "dev"),
        P(None, None, "dev"),
        P(),
        P(),
    )
    return jax.shard_map(
        on_device,
        mesh=mesh,
        in_specs=placed,
        out_specs=(P("wa", "dev"), P("wa", "dev"), P("wa", None, "dev"), P("wa", None, "dev")),
        check_vma=False,
    )
```

profile of v0, /device:TPU:2, one launch (start us, length us, event | category | flops | bytes accessed | tf_op | source)
XLA Modules:
  0.0 798.2 jit_solution(14165972701911176698)
XLA Ops:
  7.2 0.0 copy-start
  7.2 0.0 copy-start.5
  7.2 0.0 copy-start.6
  7.2 0.0 all-gather.2.cloned.1.call-start
  7.2 3.9 copy.13
  11.2 0.0 all-gather.2.cloned.1.call-update
  11.2 0.0 reduce-scatter.5.cloned.1.call-start
  11.2 0.0 copy-done.5
  11.3 0.1 dynamic_slice.11
  11.3 0.1 broadcast_in_dim.69
  11.4 0.1 reshape.82
  11.5 0.0 copy-done.6
  11.5 0.1 dynamic-slice_bitcast_fusion
  11.6 0.1 broadcast_in_dim.72
  11.6 0.1 eq.21
  11.7 0.0 copy-start.1
  11.8 0.0 copy-start.2
  11.8 0.0 copy-start.3
  11.8 1.9 broadcast_select_fusion
  13.7 0.0 copy-done.1
  13.7 0.2 fusion.5
  13.9 0.0 copy-done
  13.9 0.0 copy-done.2
  13.9 0.0 copy-done.3
  14.0 0.5 fusion.4
  14.5 52.8 %all-reduce = (bf16[128,16]{0,1:T(8,128)(2,1)S(1)}, bf16[128,16]{0,1:T(8,128)(2,1)S(1)}) all-reduce(f32[128,16]{0,1:T(8,128)S(1)} %fusion.5, f32[128,16]{0,1:T(8,128)S(1)} %fusion.4), channel_id=1, replica_groups=mesh['wa'=16,'dev'=16] {'dev'}, use_global_device_ids=true, to_apply=%region_2.3 | all-reduce | flops 4096 | bytes 24576 | tf_op jit(solution)/shard_map/psum | solution.py:79
  67.3 1.0 convolution_multiply_fusion.1
  68.3 0.0 reduce-scatter.5.cloned.1.call-update
  68.4 0.0 reduce-scatter.3.cloned.1.call-start
  68.4 2.9 convolution_multiply_fusion
  71.3 0.0 reduce-scatter.3.cloned.1.call-update
  71.3 308.6 %all-gather.2.cloned.1.call-done = bf16[1792,8192]{0,1:T(8,128)(2,1)} async-done(((bf16[1792,512]{0,1:T(8,128)(2,1)}), bf16[1792,8192]{0,1:T(8,128)(2,1)}) %all-gather.2.cloned.1.call-update) | async-done | bytes 29360144 | tf_op jit(solution)/shard_map/all_gather | solution.py:41
  379.9 16.4 %convolution_convert_fusion = bf16[16,128,1792]{2,1,0:T(8,128)(2,1)} fusion(bf16[1792,16,512]{0,2,1:T(8,128)(2,1)} %bitcast.29, bf16[16,16,8,512]{3,2,1,0:T(8,128)(2,1)S(1)} %bitcast.30), kind=kOutput, calls=%fused_computation.1 | convolution fusion | flops 3761766400 | bytes 38797312 | tf_op jit(solution)/shard_map/tkc,fkc->ktf/dot_general | solution.py:45
  396.3 0.0 copy-start.4
  396.3 4.3 convert_reduce_fusion
  400.6 0.0 copy-done.4
  400.6 1.6 fusion.15
  402.2 178.1 %reduce-scatter.5.cloned.1.call-done = f32[1,16,512]{2,1,0:T(8,128)} async-done(((f32[16,16,512]{2,1,0:T(8,128)}), f32[1,16,512]{2,1,0:T(8,128)}) %reduce-scatter.5.cloned.1.call-update) | async-done | bytes 32784 | tf_op jit(solution)/shard_map/reduce_scatter | solution.py:100
  580.3 211.3 %reduce-scatter.3.cloned.1.call-done = f32[1,16,1792]{2,1,0:T(8,128)} async-done(((f32[16,16,1792]{2,1,0:T(8,128)}), f32[1,16,1792]{2,1,0:T(8,128)}) %reduce-scatter.3.cloned.1.call-update) | async-done | bytes 114704 | tf_op jit(solution)/shard_map/reduce_scatter | solution.py:99
  (3 shorter events, 0.0 us)
Async XLA Ops:
  7.2 6.8 copy-start
  7.2 4.1 copy-start.5
  7.2 4.3 copy-start.6
  7.2 372.7 %all-gather.2.cloned.1.call-start = ((), (), s32[]{:S(2)}) async-start(), calls=%async_computation.2 | async-start | bytes 31195136 | tf_op jit(solution)/shard_map/all_gather | solution.py:41
  11.2 569.1 %reduce-scatter.5.cloned.1.call-start = ((), (), s32[]{:S(2)}) async-start(), calls=%async_computation.4 | async-start | bytes 557056 | tf_op jit(solution)/shard_map/reduce_scatter | solution.py:100
  11.7 1.9 copy-start.1
  11.8 2.2 copy-start.2
  11.8 2.2 copy-start.3
  68.4 723.3 %reduce-scatter.3.cloned.1.call-start = ((), (), s32[]{:S(2)}) async-start(), calls=%async_computation.3 | async-start | bytes 1949696 | tf_op jit(solution)/shard_map/reduce_scatter | solution.py:99
  396.3 4.3 copy-start.4
Sparse Core Ops, SparseCore 0:
  11.3 368.5 all-gather.1
  384.2 196.0 reduce-scatter.4
  584.8 206.8 reduce-scatter.2
where the time goes:
time: 798 us
  waiting for transfers between devices  698 us (87%)
  blocking collectives  52.8 us (7%)
  matrix products  22.7 us (3%)
  between operations  13.9 us (2%)
    all_gather x1, waiting for transfers between devices, on_device(): shard_piece = lax.all_gather(down_weight, 'wa', axis=1, tiled=True)  309 us
    reduce_scatter x1, waiting for transfers between devices, on_device(): lax.psum_scatter(down_factor_partial, 'wa', scatter_dimension=0, tiled=True)  211 us
    reduce_scatter x1, waiting for transfers between devices, on_device(): lax.psum_scatter(up_factor_partial, 'wa', scatter_dimension=0, tiled=True)  178 us
    psum x1, blocking collectives, on_device(): in_summed, out_summed = lax.psum((in_partial, out_partial), 'dev')  52.8 us
    dot_general x1, matrix products, on_device(): jnp.einsum('tkc,fkc->ktf', left, right, preferred_element_type=jnp.float32)  16.4 us
  transfers between devices with their start and end apart: 3, of which 3 were waited for; matrix products, arithmetic and copies ran while one was open for 4% of the time, Pallas kernels for 0%

commit v1 on v0

--- a/solution.py
+++ b/solution.py
@@ -38,7 +38,10 @@
     gate_wide = gate_preactivation.astype(jnp.float32)
     up_wide = up_preactivation.astype(jnp.float32)
     hidden_state = (jax.nn.silu(gate_wide) * up_wide).astype(jnp.bfloat16)
-    shard_piece = lax.all_gather(down_weight, "wa", axis=1, tiled=True)
+    devices = lax.axis_size("wa")
+    shards = jnp.stack([down_weight for _ in range(devices)])
+    shards = lax.all_to_all(shards, "wa", split_axis=0, concat_axis=0)
+    shard_piece = jnp.concatenate(shards, axis=1)
     groups = shard_piece.shape[1] // wa_cols
     left = masked_rows.reshape(token_rows, groups, wa_cols)
     right = shard_piece.reshape(hidden_local, groups, wa_cols)

time: 798 us -> 939 us (1.18)
  waiting for transfers between devices: 698 us -> 816 us
  starting transfers between devices: 0.12 us -> 11.5 us
    all_to_all x0 -> x1, waiting for transfers between devices: none -> 600 us  [on_device(): shards = lax.all_to_all(shards, 'wa', split_axis=0, concat_axis=0)]
    all_gather x1 -> x0, waiting for transfers between devices: 309 us -> none  [on_device(): shard_piece = lax.all_gather(down_weight, 'wa', axis=1, tiled=True)]
    reduce_scatter x1, waiting for transfers between devices: 178 us -> 0.01 us  [on_device(): lax.psum_scatter(up_factor_partial, 'wa', scatter_dimension=0, tiled=True)]
    all_to_all x0 -> x1, starting transfers between devices: none -> 11.4 us  [on_device(): shards = lax.all_to_all(shards, 'wa', split_axis=0, concat_axis=0)]
    another operation x0 -> x1, local copies, waits for them, and re-layouts: none -> 11 us  [on_device(): shards = jnp.stack([down_weight for _ in range(devices)])]
  transfers between devices with their start and end apart: 3 -> 3, of which waited for: 3 -> 2; matrix products, arithmetic and copies ran while one was open for 4% -> 3% of each run, Pallas kernels for 0% -> 0%
where the time goes in v1:
time: 939 us; the launch traced here: 938 us
  waiting for transfers between devices  816 us (87%)
  blocking collectives  55.4 us (6%)
  matrix products  23.9 us (3%)
  between operations  14.2 us (2%)
  local copies, waits for them, and re-layouts  11.5 us (1%)
  starting transfers between devices  11.5 us (1%)
    all_to_all x1, waiting for transfers between devices, on_device(): shards = lax.all_to_all(shards, 'wa', split_axis=0, concat_axis=0)  600 us
    reduce_scatter x1, waiting for transfers between devices, on_device(): lax.psum_scatter(down_factor_partial, 'wa', scatter_dimension=0, tiled=True)  215 us
    psum x1, blocking collectives, on_device(): in_summed, out_summed = lax.psum((in_partial, out_partial), 'dev')  55.4 us
  transfers between devices with their start and end apart: 3, of which 2 were waited for; matrix products, arithmetic and copies ran while one was open for 3% of the time, Pallas kernels for 0%

profile of v1, /device:TPU:2, one launch (start us, length us, event | category | flops | bytes accessed | tf_op | source)
XLA Modules:
  0.0 938.4 jit_solution(10958148752287580725)
XLA Ops:
  7.2 0.0 copy-start
  7.2 11.0 %stack.2 = bf16[16,1792,512]{2,1,0:T(8,128)(2,1)} broadcast(bf16[1792,512]{1,0:T(8,128)(2,1)} %param.9), dimensions={1,2} | broadcast | bytes 31195136 | tf_op jit(solution)/shard_map/stack | solution.py:42
  18.2 0.0 copy-start.5
  18.2 0.0 copy-start.6
  18.2 11.4 %all-to-all-start = ((bf16[16,1792,512]{2,1,0:T(8,128)(2,1)}), bf16[16,1792,512]{2,1,0:T(8,128)(2,1)}, u32[]{:S(2)}, u32[]{:S(2)}) async-start(bf16[16,1792,512]{2,1,0:T(8,128)(2,1)} %stack.2), calls=%async_computation | async-start | bytes 58720256 | tf_op jit(solution)/shard_map/all_to_all | solution.py:43
  29.6 0.0 reduce-scatter.5.cloned.1.call-start
  29.7 0.0 copy-done.5
  29.7 0.1 dynamic_slice.11
  29.8 0.1 broadcast_in_dim.69
  29.8 0.1 reshape.84
  29.9 0.0 copy-done.6
  29.9 0.1 dynamic-slice_bitcast_fusion
  30.0 0.1 broadcast_in_dim.72
  30.1 0.1 eq.21
  30.2 0.0 copy-start.1
  30.2 0.0 copy-start.2
  30.2 0.0 copy-start.3
  30.2 1.9 broadcast_select_fusion
  32.1 0.0 copy-done.1
  32.1 0.2 fusion.10
  32.4 0.0 copy-done
  32.4 0.0 copy-done.2
  32.4 0.0 copy-done.3
  32.4 0.5 fusion.9
  32.9 55.4 %all-reduce = (bf16[128,16]{0,1:T(8,128)(2,1)S(1)}, bf16[128,16]{0,1:T(8,128)(2,1)S(1)}) all-reduce(f32[128,16]{0,1:T(8,128)S(1)} %fusion.10, f32[128,16]{0,1:T(8,128)S(1)} %fusion.9), channel_id=1, replica_groups=mesh['wa'=16,'dev'=16] {'dev'}, use_global_device_ids=true, to_apply=%region_2.3 | all-reduce | flops 4096 | bytes 24576 | tf_op jit(solution)/shard_map/psum | solution.py:82
  88.4 1.1 convolution_multiply_fusion.1
  89.4 0.0 reduce-scatter.5.cloned.1.call-update
  89.4 0.0 reduce-scatter.3.cloned.1.call-start
  89.5 2.8 convolution_multiply_fusion
  92.3 0.0 reduce-scatter.3.cloned.1.call-update
  92.3 600.5 %all-to-all-done = bf16[16,1792,512]{2,1,0:T(8,128)(2,1)} async-done(((bf16[16,1792,512]{2,1,0:T(8,128)(2,1)}), bf16[16,1792,512]{2,1,0:T(8,128)(2,1)}, u32[]{:S(2)}, u32[]{:S(2)}) %all-to-all-start) | async-done | bytes 29360160 | tf_op jit(solution)/shard_map/all_to_all | solution.py:43
  692.8 17.7 %fusion.2 = bf16[16,128,1792]{2,1,0:T(8,128)(2,1)} fusion(bf16[16,1792,512]{2,1,0:T(8,128)(2,1)} %all-to-all-done, bf16[16,16,8,512]{3,2,1,0:T(8,128)(2,1)S(1)} %bitcast.32), kind=kOutput, calls=%fused_computation.3 | convolution fusion | flops 3761766400 | bytes 38797312 | tf_op jit(solution)/shard_map/tkc,fkc->ktf/dot_general | solution.py:48
  710.5 0.0 copy-start.4
  710.5 4.3 convert_reduce_fusion
  714.8 0.0 copy-done.4
  714.8 1.6 fusion.20
  716.4 0.0 reduce-scatter.5.cloned.1.call-done
  716.4 215.2 %reduce-scatter.3.cloned.1.call-done = f32[1,16,1792]{2,1,0:T(8,128)} async-done(((f32[16,16,1792]{2,1,0:T(8,128)}), f32[1,16,1792]{2,1,0:T(8,128)}) %reduce-scatter.3.cloned.1.call-update) | async-done | bytes 114704 | tf_op jit(solution)/shard_map/reduce_scatter | solution.py:102
  (3 shorter events, 0.0 us)
Async XLA Ops:
  7.2 25.2 %copy-start = (bf16[16,16,1792]{2,1,0:T(8,128)(2,1)S(1)}, bf16[16,16,1792]{2,1,0:T(8,128)(2,1)}, u32[]{:S(2)}) copy-start(bf16[16,16,1792]{2,1,0:T(8,128)(2,1)} %param.12) | copy-start | bytes 2752516
  18.2 11.5 %copy-start.5 = (s32[128]{0:T(128)S(1)}, s32[128]{0:T(128)}, u32[]{:S(2)}) copy-start(s32[128]{0:T(128)} %param.15) | copy-start | bytes 1540
  18.2 11.7 %copy-start.6 = (s32[128,1]{0,1:T(1,128)S(1)}, s32[128,1]{0,1:T(1,128)}, u32[]{:S(2)}) copy-start(s32[128,1]{0,1:T(1,128)} %param.14) | copy-start | bytes 1540
  18.2 674.6 %all-to-all-start = ((bf16[16,1792,512]{2,1,0:T(8,128)(2,1)}), bf16[16,1792,512]{2,1,0:T(8,128)(2,1)}, u32[]{:S(2)}, u32[]{:S(2)}) async-start(bf16[16,1792,512]{2,1,0:T(8,128)(2,1)} %stack.2), calls=%async_computation | async-start | bytes 58720256 | tf_op jit(solution)/shard_map/all_to_all | solution.py:43
  29.6 686.8 %reduce-scatter.5.cloned.1.call-start = ((), (), s32[]{:S(2)}) async-start(), calls=%async_computation.4 | async-start | bytes 557056 | tf_op jit(solution)/shard_map/reduce_scatter | solution.py:103
  30.2 1.9 copy-start.1
  30.2 2.2 copy-start.2
  30.2 2.2 copy-start.3
  89.4 842.1 %reduce-scatter.3.cloned.1.call-start = ((), (), s32[]{:S(2)}) async-start(), calls=%async_computation.3 | async-start | bytes 1949696 | tf_op jit(solution)/shard_map/reduce_scatter | solution.py:102
  710.5 4.3 copy-start.4
Sparse Core Ops, SparseCore 0:
  89.6 619.3 reduce-scatter.4
  713.4 218.1 reduce-scatter.2
